TPU v7x, 32 devices: a whole 2x2x4 slice. The times are simulated.
32 devices in a mesh: aux: 4 (over y, x), blk: 8 (over z, core).
Axes of the slice: x: 2, y: 2, z: 4, core: 2. Of those that a mesh axis runs over, the one named last changes fastest.
Arguments:
- three_center: bfloat16 [384, 4, 128, 128], P(('aux', 'blk')), may hold values from -6 to 6
- slot_block: int32 [384], P(('aux', 'blk')), may hold values from 0 to 47
- slot_aux: int32 [384], P(('aux', 'blk')), may hold values from 0 to 1
- live_slots: int32 [32], P(('aux', 'blk')), may hold values from 1 to 12, as said below
- vir_coef: bfloat16 [6144, 256], replicated, may hold values from -0.00478416 to 0.00478416
- eps_occ: float32 [4000], replicated, may hold values from -1.5 to -0.3
- eps_vir: float32 [256], replicated, may hold values from 0.2 to 3
- occ_index: int32 [4], replicated, may hold values from 0 to 3999, as said below
Outputs:
- amplitudes: float32 [4, 256, 4, 256], P('aux', 'blk')
- pair_energy: float32 [4, 4], P('aux')
Inputs may be any that keep to these rules, and one draw needn't show every extreme that they name: The slots in use on a device are its first live_slots ones; the others hold data that is not used. Some device holds exactly 12 slots in use in every draw. `occ_index`: the indices are distinct; the first and the last occupied orbital of the system are in every batch.
All inputs are finite; a program needn't handle non-finite values.
Results may differ from a plain program's by a relative error of at most 0.0035.
Values may be sent and summed in bfloat16 or wider, within the bound.
A program may use at most 64 MiB of HBM per device.

v0:
```python
import jax
import jax.numpy as jnp
from jax import lax
from jax.sharding import PartitionSpec as P

AUX_BLOCKS_DEV = 2


def body(three_center, slot_block, slot_aux, live_slots, vir_coef, eps_occ, eps_vir, occ_index):
    blk_count = lax.axis_size("blk")
    occ_row = lax.axis_index("aux")
    slot_count = three_center.shape[0]
    occ_count = three_center.shape[1]
    ao_span = three_center.shape[3]
    vir_count = vir_coef.shape[1]
    coef_blocks = vir_coef.reshape(vir_coef.shape[0] // ao_span, ao_span, vir_count)
    coefficients = jnp.take(coef_blocks, slot_block, axis=0)
    products = jnp.einsum(
        "soqn,snv->soqv", three_center, coefficients, preferred_element_type=jnp.float32
    )
    keep = (jnp.arange(slot_count) < live_slots[0]).astype(jnp.float32)
    select = (slot_aux[:, None] == jnp.arange(AUX_BLOCKS_DEV)[None, :]).astype(jnp.float32)
    select = select * keep[:, None]
    local_rows = jnp.einsum("sk,soqv->kqov", select, products).astype(jnp.bfloat16)
    halfed = lax.all_gather(local_rows, "aux", axis=0, tiled=True)
    own_rows = lax.dynamic_index_in_dim(halfed, occ_row, 2, keepdims=False)
    rows_dev = vir_count // blk_count
    mixed = lax.dot_general(
        halfed, own_rows, (((0, 1), (0, 1)), ((), ())), preferred_element_type=jnp.float32
    )
    summed = lax.psum_scatter(
        jnp.stack(
            [
                lax.dot_general(
                    own_rows,
                    halfed,
                    (((0, 1), (0, 1)), ((), ())),
                    preferred_element_type=jnp.float32,
                ),
                jnp.transpose(mixed, (1, 0, 2)),
            ],
            axis=1,
        ),
        "blk",
        scatter_dimension=0,
        tiled=True,
    )
    direct = summed[:, 0]
    crossed = summed[:, 1]
    first_vir = lax.axis_index("blk") * rows_dev
    occ_levels = jnp.take(eps_occ, occ_index)
    own_level = jnp.sum(jnp.where(jnp.arange(occ_count) == occ_row, occ_levels, 0.0))
    vir_levels = lax.dynamic_slice_in_dim(eps_vir, first_vir, rows_dev, 0)
    denominator = (
        own_level + occ_levels[None, :, None] - vir_levels[:, None, None] - eps_vir[None, None, :]
    )
    amplitudes = (direct / denominator)[None]
    pair_part = jnp.sum(direct * (2.0 * direct - crossed) / denominator, axis=(0, 2))
    pair_energy = lax.psum(pair_part, "blk")[None]
    return (amplitudes, pair_energy)


def solution(mesh):
    in_specs = (
        P(("aux", "blk"), None, None, None),
        P(("aux", "blk")),
        P(("aux", "blk")),
        P(("aux", "blk")),
        P(),
        P(),
        P(),
        P(),
    )
    out_specs = (P("aux", "blk", None, None), P("aux", None))
    return jax.shard_map(body, mesh=mesh, in_specs=in_specs, out_specs=out_specs, check_vma=False)
```

profile of v0, /device:TPU:0, one launch (start us, length us, event | category | flops | bytes accessed | tf_op | source)
XLA Modules:
  0.0 131.5 jit_solution(10336060481008152967)
XLA Ops:
  7.2 0.0 copy-start
  7.2 0.0 all-gather.2.cloned.1.call-start
  7.2 0.8 compare_select_fusion.1
  8.0 0.8 compare_and_fusion
  8.8 0.3 copy-done
  9.1 1.5 %gather_fusion = bf16[12,128,256]{2,1,0:T(8,128)(2,1)} fusion(bf16[48,128,256]{2,1,0:T(8,128)(2,1)S(1)} %bitcast.68, s32[1024]{0:T(1024)S(1)} %pad_clamp_fusion.1), kind=kCustom, calls=%fused_computation | custom fusion | bytes 1572912 | tf_op jit(solution)/shard_map/jit(_take)/gather | solution.py:17
  10.6 4.8 %convolution_bitcast_fusion = bf16[12,4,128,256]{2,3,1,0:T(8,128)(2,1)} fusion(bf16[12,4,128,128]{3,2,1,0:T(8,128)(2,1)} %param.8, bf16[12,128,256]{2,1,0:T(8,128)(2,1)} %gather_fusion, pred[12]{0:T(512)(128)(4,1)S(1)} %compare_and_fusion), kind=kOutput, calls=%fused_computation.2 | convolution fusion | flops 403046400 | bytes 5505036 | tf_op jit(solution)/shard_map/soqn,snv->soqv/dot_general | solution.py:18
  15.4 0.0 copy-start.4
  15.4 7.7 %copy.28 = bf16[12,4,128,256]{3,0,2,1:T(8,128)(2,1)} copy(bf16[12,4,128,256]{2,3,1,0:T(8,128)(2,1)} %convolution_bitcast_fusion) | data formatting | bytes 6291456 | tf_op jit(solution)/shard_map/soqn,snv->soqv/dot_general | solution.py:18
  23.7 0.0 copy-done.4
  23.7 2.9 %fusion = bf16[2,128,4,256]{3,0,1,2:T(2,128)(2,1)S(1)} fusion(bf16[12,4,128,256]{3,0,2,1:T(8,128)(2,1)} %copy.28, bf16[12]{0:T(256)(128)(2,1)S(1)} %compare_convert_fusion, s32[12]{0:T(128)S(1)} %copy-done.4), kind=kOutput, calls=%fused_computation.7 | convolution fusion | flops 6291504 | bytes 3670088 | tf_op jit(solution)/shard_map/sk,soqv->kqov/dot_general | solution.py:24
  26.6 0.9 copy.29
  27.5 0.0 all-gather.2.cloned.1.call-update
  27.5 0.0 reduce-scatter.2.cloned.1.call-start
  27.6 38.0 %all-gather.2.cloned.1.call-done = bf16[8,128,4,256]{3,1,2,0:T(8,128)(2,1)} async-done(((bf16[2,128,4,256]{3,1,2,0:T(8,128)(2,1)}), bf16[8,128,4,256]{3,1,2,0:T(8,128)(2,1)}) %all-gather.2.cloned.1.call-update) | async-done | bytes 2097168 | tf_op jit(solution)/shard_map/all_gather | solution.py:25
  65.6 0.0 copy-start.5
  65.6 2.6 %convolution_bitcast_fusion.2 = f32[256,1,4,256]{3,0,2,1:T(8,128)S(1)} fusion(bf16[8,128,4,256]{3,1,2,0:T(8,128)(2,1)} %all-gather.2.cloned.1.call-done, s32[]{:T(128)S(6)} %select_n.33), kind=kOutput, calls=%fused_computation.5 | convolution fusion | flops 536870912 | bytes 3670020 | tf_op jit(solution)/shard_map/dot_general | solution.py:28
  68.2 0.0 copy-done.5
  68.2 0.7 convolution_bitcast_fusion.1
  68.9 1.5 %pad_maximum_fusion = f32[256,2,4,256]{3,0,2,1:T(8,128)} fusion(f32[256,1,4,256]{3,0,2,1:T(8,128)S(1)} %convolution_bitcast_fusion.2, f32[256,1,4,256]{3,0,2,1:T(8,128)S(1)} %convolution_bitcast_fusion.1), kind=kLoop, calls=%fused_computation.3 | loop fusion | flops 524288 | bytes 4194304 | tf_op jit(solution)/shard_map/stack | solution.py:32
  70.4 0.0 copy-start.2
  70.4 0.0 copy-start.3
  70.4 0.0 copy-start.1
  70.4 0.0 reduce-scatter.2.cloned.1.call-update
  70.4 0.6 copy-done.2
  71.1 0.1 dynamic_slice.8
  71.2 0.0 copy-done.3
  71.2 0.0 copy-done.1
  71.2 0.6 gather_fusion.1
  71.8 0.6 fusion.16
  72.4 0.7 broadcast_add_fusion
  73.1 0.1 broadcast_subtract_fusion
  73.2 33.5 %reduce-scatter.2.cloned.1.call-done = f32[32,2,4,256]{3,0,2,1:T(8,128)} async-done(((f32[256,2,4,256]{3,0,2,1:T(8,128)}), f32[32,2,4,256]{3,0,2,1:T(8,128)}) %reduce-scatter.2.cloned.1.call-update) | async-done | bytes 262160 | tf_op jit(solution)/shard_map/reduce_scatter | solution.py:31
  106.7 1.0 bitcast_divide_fusion
  107.7 0.7 copy.34
  108.4 1.2 fusion.12
  109.6 15.1 %psum.7 = f32[1,4]{1,0:T(1,128)} all-reduce(f32[1,4]{1,0:T(1,128)S(1)} %bitcast.69), channel_id=1, replica_groups=mesh['aux'=4,'blk'=8] {'blk'}, use_global_device_ids=true, to_apply=%region_3.4 | all-reduce | flops 4 | bytes 32 | tf_op jit(solution)/shard_map/psum | solution.py:59
  (4 shorter events, 0.0 us)
Async XLA Ops:
  7.2 1.9 %copy-start = (bf16[6144,256]{1,0:T(8,128)(2,1)S(1)}, bf16[6144,256]{1,0:T(8,128)(2,1)}, u32[]{:S(2)}) copy-start(bf16[6144,256]{1,0:T(8,128)(2,1)} %param.12) | copy-start | bytes 9437188
  7.2 58.4 %all-gather.2.cloned.1.call-start = ((), (), s32[]{:S(2)}) async-start(), calls=%async_computation.1 | async-start | bytes 2621440 | tf_op jit(solution)/shard_map/all_gather | solution.py:25
  15.4 8.4 %copy-start.4 = (s32[12]{0:T(128)S(1)}, s32[12]{0:T(128)}, u32[]{:S(2)}) copy-start(s32[12]{0:T(128)} %param.10) | copy-start | bytes 148
  27.5 79.1 %reduce-scatter.2.cloned.1.call-start = ((), (), s32[]{:S(2)}) async-start(), calls=%async_computation.2 | async-start | bytes 2359296 | tf_op jit(solution)/shard_map/reduce_scatter | solution.py:31
  65.6 2.6 %copy-start.5 = (bf16[8,128,4,256]{3,1,2,0:T(8,128)(2,1)S(1)}, bf16[8,128,4,256]{3,1,2,0:T(8,128)(2,1)}, u32[]{:S(2)}) copy-start(bf16[8,128,4,256]{3,1,2,0:T(8,128)(2,1)} %all-gather.2.cloned.1.call-done) | copy-start | bytes 6291460
  70.4 0.7 copy-start.2
  70.4 0.8 copy-start.3
  70.4 0.8 copy-start.1
Sparse Core Ops, SparseCore 0:
  27.6 37.8 all-gather.1
  70.6 36.0 reduce-scatter.1
where the time goes:
time: 132 us; the launch traced here: 131 us
  waiting for transfers between devices  71.6 us (54%)
  blocking collectives  15.1 us (11%)
  between operations  14.8 us (11%)
  local copies, waits for them, and re-layouts  12.5 us (9%)
  matrix products  11 us (8%)
  other arithmetic  6.57 us (5%)
    all_gather x1, waiting for transfers between devices, body(): halfed = lax.all_gather(local_rows, 'aux', axis=0, tiled=True)  38 us
    reduce_scatter x1, waiting for transfers between devices, body(): lax.psum_scatter(jnp.stack([lax.dot_general(own_rows, halfed, (((0, 1), (...  33.5 us
    psum x1, blocking collectives, body(): pair_energy = lax.psum(pair_part, 'blk')[None]  15.1 us
    dot_general x1, local copies, waits for them, and re-layouts, body(): jnp.einsum('soqn,snv->soqv', three_center, coefficients, preferred_elemen...  7.69 us
    dot_general x1, matrix products, body(): jnp.einsum('soqn,snv->soqv', three_center, coefficients, preferred_elemen...  4.8 us
    dot_general x1, matrix products, body(): jnp.einsum('sk,soqv->kqov', select, products).astype(jnp.bfloat16)  2.88 us
  transfers between devices with their start and end apart: 2, of which 2 were waited for; matrix products, arithmetic and copies ran while one was open for 2% of the time, Pallas kernels for 0%

commit v1 on v0

v1 whole, which is shorter than its diff:
```python
import functools

import jax
import jax.numpy as jnp
from jax import lax
from jax.experimental import pallas as pl
from jax.experimental.pallas import tpu as pltpu
from jax.sharding import PartitionSpec as P

AUX_BLOCKS_DEV = 2
MESH = pl.DeviceIdType.MESH
LANES = 128


def half_kernel(slots, occ, block_ref, aux_ref, live_ref, index_ref, tc_hbm, coef_hbm, eps_hbm,
                h_ref, level_ref, tc_buf, coef_buf, acc, eps_buf, tc_sem, coef_sem, eps_sem):
    span = coef_buf.shape[1]
    rows = tc_buf.shape[1] // occ
    vir = coef_buf.shape[2]
    eps_copy = pltpu.make_async_copy(eps_hbm, eps_buf, eps_sem)
    copies = []
    for s in range(slots):
        start = pl.multiple_of(block_ref[s] * span, span)
        copies.append((
            pltpu.make_async_copy(tc_hbm.at[s], tc_buf.at[s], tc_sem.at[s]),
            pltpu.make_async_copy(coef_hbm.at[pl.ds(start, span)], coef_buf.at[s], coef_sem.at[s]),
        ))
        for c in copies[-1]:
            c.start()
    eps_copy.start()
    acc[...] = jnp.zeros_like(acc)
    for s in range(slots):
        for c in copies[s]:
            c.wait()

        @pl.when(s < live_ref[0])
        def _():
            acc[aux_ref[s]] += jnp.dot(tc_buf[s], coef_buf[s], preferred_element_type=jnp.float32)

    for k in range(AUX_BLOCKS_DEV):
        for i in range(occ):
            h_ref[k * rows:(k + 1) * rows, i * vir:(i + 1) * vir] = (
                acc[k, i * rows:(i + 1) * rows, :].astype(jnp.bfloat16))
    eps_copy.wait()
    for i in range(occ):
        level_ref[i] = eps_buf[index_ref[i]]


def pair_kernel(na, nb, h_ref, level_ref, eps_ref, amp_ref, e_ref,
                held, part, core_in, out_z, in_z, turned, tiles, e_own, e_all,
                g_send, g_recv, c_send, c_recv, z_send, z_recv, t_send, t_recv, e_send, e_recv):
    me = lax.axis_index("aux")
    blk = lax.axis_index("blk")
    nz = nb // 2
    core = lax.rem(blk, 2)
    zed = lax.div(blk, 2)
    vir = eps_ref.shape[1]
    rows = vir // nb

    def aux_peer(d):
        return (lax.rem(me + d, na), blk)

    def blk_peer(d):
        return (me, lax.rem(blk + d, nb))

    def z_peer(d):
        return (me, 2 * lax.rem(zed + d, nz) + core)

    barrier = pltpu.get_barrier_semaphore()
    for d in range(1, na):
        pl.semaphore_signal(barrier, inc=1, device_id=aux_peer(d), device_id_type=MESH)
    for d in range(1, nb):
        pl.semaphore_signal(barrier, inc=1, device_id=blk_peer(d), device_id_type=MESH)
    pl.semaphore_wait(barrier, na + nb - 2)

    gathers = []
    for d in range(1, na):
        gathers.append(pltpu.make_async_remote_copy(
            src_ref=h_ref, dst_ref=held.at[d - 1], send_sem=g_send.at[d - 1], recv_sem=g_recv.at[d - 1],
            device_id=aux_peer(d), device_id_type=MESH))
        gathers[-1].start()

    own_cols = pl.ds(pl.multiple_of(me * vir, vir), vir)

    def add(src, first):
        left = jnp.transpose(src[:, own_cols])
        for j in range(na):
            cols = slice(j * vir, (j + 1) * vir)
            res = jnp.dot(left, src[:, cols], preferred_element_type=jnp.float32)
            for k in range(nb):
                piece = res[k * rows:(k + 1) * rows]
                if first:
                    part[k % 2, k // 2, :, cols] = piece
                else:
                    part[k % 2, k // 2, :, cols] += piece

    add(h_ref, True)
    for d in range(1, na):
        gathers[d - 1].wait_recv()
        add(held.at[d - 1], False)

    swap = pltpu.make_async_remote_copy(
        src_ref=part.at[1 - core], dst_ref=core_in, send_sem=c_send, recv_sem=c_recv,
        device_id=(me, 2 * zed + 1 - core), device_id_type=MESH)
    swap.start()
    swap.wait_recv()
    sends = []
    for d in range(1, nz):
        to = lax.rem(zed + d, nz)
        out_z[d - 1] = (part[core, to] + core_in[to]).astype(jnp.bfloat16)
        sends.append(pltpu.make_async_remote_copy(
            src_ref=out_z.at[d - 1], dst_ref=in_z.at[d - 1], send_sem=z_send.at[d - 1],
            recv_sem=z_recv.at[d - 1], device_id=z_peer(d), device_id_type=MESH))
        sends[-1].start()
    total = part[core, zed] + core_in[zed]
    for d in range(1, nz):
        sends[d - 1].wait_recv()
        total = total + in_z[d - 1].astype(jnp.float32)

    pieces = [total[:, j * vir:(j + 1) * vir] for j in range(na)]
    stacked = pieces
    if na * rows < LANES:
        stacked = pieces + [jnp.zeros((LANES - na * rows, vir), jnp.float32)]
    turned[...] = jnp.transpose(jnp.concatenate(stacked, axis=0))
    swaps = []
    for d in range(1, nb):
        to = lax.rem(blk + d, nb)
        swaps.append(pltpu.make_async_remote_copy(
            src_ref=turned.at[pl.ds(pl.multiple_of(to * rows, rows), rows)], dst_ref=tiles.at[blk],
            send_sem=t_send.at[d - 1], recv_sem=t_recv.at[d - 1],
            device_id=blk_peer(d), device_id_type=MESH))
        swaps[-1].start()
    tiles[blk] = turned[pl.ds(pl.multiple_of(blk * rows, rows), rows), :]

    level = eps_ref[...]
    turn = jnp.transpose(jnp.broadcast_to(level, (LANES, vir)))
    own_level = level_ref[me]
    column = jnp.zeros((rows, LANES), jnp.float32)
    for k in range(nb):
        column = jnp.where(blk == k, turn[k * rows:(k + 1) * rows], column)
    column = column[:, :1]
    ratios = []
    for j in range(na):
        ratio = pieces[j] / (((own_level + level_ref[j]) - column) - level)
        amp_ref[:, j * vir:(j + 1) * vir] = ratio
        ratios.append(ratio)

    for c in swaps:
        c.wait_recv()
    lane = lax.broadcasted_iota(jnp.int32, (rows, LANES), 1)
    lane_e = lax.broadcasted_iota(jnp.int32, (8, LANES), 1)
    per = LANES // rows
    energy = jnp.zeros((8, LANES), jnp.float32)
    for j in range(na):
        groups = []
        for g in range(vir // LANES):
            crossed = jnp.zeros((rows, LANES), jnp.float32)
            for m in range(per):
                tile = tiles[g * per + m]
                shift = (rows * (m - j)) % LANES
                if shift:
                    tile = pltpu.roll(tile, shift, 1)
                crossed = jnp.where(lax.div(lane, rows) == m, tile, crossed)
            groups.append(crossed)
        crossed = jnp.concatenate(groups, axis=1)
        value = jnp.sum(ratios[j] * (2.0 * pieces[j] - crossed))
        energy = jnp.where(lane_e == j, value, energy)
    e_own[...] = energy
    e_all[blk] = energy
    e_sends = []
    for d in range(1, nb):
        e_sends.append(pltpu.make_async_remote_copy(
            src_ref=e_own, dst_ref=e_all.at[blk], send_sem=e_send.at[d - 1], recv_sem=e_recv.at[d - 1],
            device_id=blk_peer(d), device_id_type=MESH))
        e_sends[-1].start()
    for c in e_sends:
        c.wait_recv()
    result = e_all[0]
    for k in range(1, nb):
        result = result + e_all[k]
    e_ref[...] = result[:1, :na]
    for c in gathers + [swap] + sends + swaps + e_sends:
        c.wait_send()


def body(three_center, slot_block, slot_aux, live_slots, vir_coef, eps_occ, eps_vir, occ_index):
    na = lax.axis_size("aux")
    nb = lax.axis_size("blk")
    nz = nb // 2
    slots, occ, aux_rows, span = three_center.shape
    vir = vir_coef.shape[1]
    depth = AUX_BLOCKS_DEV * aux_rows
    wide = occ * vir
    rows = vir // nb
    smem = pl.BlockSpec(memory_space=pltpu.SMEM)
    vmem = pl.BlockSpec(memory_space=pltpu.VMEM)
    anyspace = pl.BlockSpec(memory_space=pl.ANY)
    half, levels = pl.pallas_call(
        functools.partial(half_kernel, slots, occ),
        out_shape=(jax.ShapeDtypeStruct((depth, wide), jnp.bfloat16),
                   jax.ShapeDtypeStruct((occ,), jnp.float32)),
        in_specs=[smem] * 4 + [anyspace] * 3,
        out_specs=(vmem, smem),
        scratch_shapes=[
            pltpu.VMEM((slots, occ * aux_rows, span), jnp.bfloat16),
            pltpu.VMEM((slots, span, vir), jnp.bfloat16),
            pltpu.VMEM((AUX_BLOCKS_DEV, occ * aux_rows, vir), jnp.float32),
            pltpu.SMEM((eps_occ.shape[0],), jnp.float32),
            pltpu.SemaphoreType.DMA((slots,)),
            pltpu.SemaphoreType.DMA((slots,)),
            pltpu.SemaphoreType.DMA,
        ],
    )(slot_block, slot_aux, live_slots, occ_index,
      three_center.reshape(slots, occ * aux_rows, span), vir_coef, eps_occ)
    dma = pltpu.SemaphoreType.DMA
    amp, energy = pl.pallas_call(
        functools.partial(pair_kernel, na, nb),
        out_shape=(jax.ShapeDtypeStruct((rows, wide), jnp.float32),
                   jax.ShapeDtypeStruct((1, na), jnp.float32)),
        in_specs=[vmem, smem, vmem],
        out_specs=(vmem, vmem),
        scratch_shapes=[
            pltpu.VMEM((na - 1, depth, wide), jnp.bfloat16),
            pltpu.VMEM((2, nz, rows, wide), jnp.float32),
            pltpu.VMEM((nz, rows, wide), jnp.float32),
            pltpu.VMEM((nz - 1, rows, wide), jnp.bfloat16),
            pltpu.VMEM((nz - 1, rows, wide), jnp.bfloat16),
            pltpu.VMEM((vir, LANES), jnp.float32),
            pltpu.VMEM((nb, rows, LANES), jnp.float32),
            pltpu.VMEM((8, LANES), jnp.float32),
            pltpu.VMEM((nb, 8, LANES), jnp.float32),
            dma((na - 1,)), dma((na - 1,)), dma, dma, dma((nz - 1,)), dma((nz - 1,)),
            dma((nb - 1,)), dma((nb - 1,)), dma((nb - 1,)), dma((nb - 1,)),
        ],
        compiler_params=pltpu.CompilerParams(collective_id=0, has_side_effects=True),
    )(half, levels, eps_vir.reshape(1, vir))
    return amp.reshape(1, rows, occ, vir), energy


def solution(mesh):
    in_specs = (
        P(("aux", "blk"), None, None, None),
        P(("aux", "blk")),
        P(("aux", "blk")),
        P(("aux", "blk")),
        P(),
        P(),
        P(),
        P(),
    )
    out_specs = (P("aux", "blk", None, None), P("aux", None))
    return jax.shard_map(body, mesh=mesh, in_specs=in_specs, out_specs=out_specs, check_vma=False)
```

time: 132 us -> 57.5 us (0.44)
  waiting for transfers between devices: 71.6 us -> 0 us
  Pallas kernels: 0 us -> 53.1 us
  blocking collectives: 15.1 us -> 0 us
  between operations: 14.8 us -> 1.29 us
  matrix products: 11 us -> 0 us
  local copies, waits for them, and re-layouts: 12.5 us -> 2.76 us
  other arithmetic: 6.57 us -> 0 us
    pallas_call x0 -> x2, Pallas kernels: none -> 53.1 us  [the longest x1 49.6 us: body(): pl.pallas_call(functools.partial(pair_kernel, na, nb), out_shape=(jax.Sha...]
    all_gather x1 -> x0, waiting for transfers between devices: 38 us -> none  [body(): halfed = lax.all_gather(local_rows, 'aux', axis=0, tiled=True)]
    reduce_scatter x1 -> x0, waiting for transfers between devices: 33.5 us -> none  [body(): lax.psum_scatter(jnp.stack([lax.dot_general(own_rows, halfed, (((0, 1), (...]
    psum x1 -> x0, blocking collectives: 15.1 us -> none  [body(): pair_energy = lax.psum(pair_part, 'blk')[None]]
    dot_general x4 -> x0, matrix products: 11 us -> none  [the longest x1 4.8 us: body(): jnp.einsum('soqn,snv->soqv', three_center, coefficients, preferred_elemen...]
    dot_general x1 -> x0, local copies, waits for them, and re-layouts: 7.69 us -> none  [body(): jnp.einsum('soqn,snv->soqv', three_center, coefficients, preferred_elemen...]
    gather x2 -> x0, local copies, waits for them, and re-layouts: 2.14 us -> none  [the longest x1 1.5 us: body(): coefficients = jnp.take(coef_blocks, slot_block, axis=0)]
    reduce_sum x2 -> x0, other arithmetic: 1.77 us -> none  [the longest x1 1.16 us: body(): jnp.sum(direct * (2.0 * direct - crossed) / denominator, axis=(0, 2))]
  transfers between devices with their start and end apart: 2 -> 0, of which waited for: 2 -> 0; matrix products, arithmetic and copies ran while one was open for 2% -> 0% of each run, Pallas kernels for 0% -> 0%
where the time goes in v1:
time: 57.5 us; the launch traced here: 57.1 us
  Pallas kernels  53.1 us (92%)
  local copies, waits for them, and re-layouts  2.76 us (5%)
  between operations  1.29 us (2%)
    pallas_call x1, Pallas kernels, body(): pl.pallas_call(functools.partial(pair_kernel, na, nb), out_shape=(jax.Sha...  49.6 us
    pallas_call x1, Pallas kernels, body(): pl.pallas_call(functools.partial(half_kernel, slots, occ), out_shape=(jax...  3.44 us
    reshape x1, local copies, waits for them, and re-layouts, body(): return (amp.reshape(1, rows, occ, vir), energy)  1.62 us

profile of v1, /device:TPU:0, one launch (start us, length us, event | category | flops | bytes accessed | tf_op | source)
XLA Modules:
  0.0 57.1 jit_solution(11723243046550955094)
XLA Ops:
  1.3 3.4 %shard_map.95 = (bf16[256,1024]{1,0:T(8,128)(2,1)}, f32[4]{0:T(128)}) custom-call(s32[12]{0:T(128)} %block_ref.1, s32[12]{0:T(128)} %aux_ref.1, s32[1]{0:T(128)S(6)} %copy.11.live_ref, s32[4]{0:T(128)} %index_ref.1, bf16[12,512,128]{2,1,0:T(8,128)(2,1)} %bitcast.2, bf16[6144,256]{1,0:T(8,128)(2,1)} %coef_hbm.1, f32[4000]{0:T(1024)} %eps_hbm.1), custom_call_target="tpu_custom_call" | custom-call | tf_op jit(solution)/shard_map/pallas_call | solution.py:198
  4.7 49.6 %shard_map.96 = (f32[32,1024]{1,0:T(8,128)}, f32[1,4]{1,0:T(1,128)}) custom-call(bf16[256,1024]{1,0:T(8,128)(2,1)} %get-tuple-element.6.h_ref, f32[4]{0:T(128)} %get-tuple-element.7.level_ref, f32[1,256]{1,0:T(1,128)} %bitcast.3), custom_call_target="tpu_custom_call" | custom-call | tf_op jit(solution)/shard_map/pallas_call | solution.py:216
  54.4 1.6 %reshape.15 = f32[1,32,4,256]{3,2,1,0:T(4,128)} reshape(f32[32,1024]{1,0:T(8,128)} %get-tuple-element.8) | data formatting | bytes 262144 | tf_op jit(solution)/shard_map/reshape | solution.py:237
  56.0 1.1 %copy.12 = f32[1,4]{1,0:T(1,128)} copy(f32[1,4]{1,0:T(1,128)} %get-tuple-element.13) | data formatting | bytes 32

commit v2 on v1

v2 whole, which is shorter than its diff:
```python
import functools

import jax
import jax.numpy as jnp
from jax import lax
from jax.experimental import pallas as pl
from jax.experimental.pallas import tpu as pltpu
from jax.sharding import PartitionSpec as P

AUX_BLOCKS_DEV = 2
MESH = pl.DeviceIdType.MESH
LANES = 128


def pair_kernel(na, nb, slots, block_ref, aux_ref, live_ref, index_ref, tc_hbm, coef_hbm, eps_hbm, eps_ref,
                amp_ref, e_ref,
                tc_buf, coef_buf, weights, eps_buf, half, held, part, core_in, out_z, in_z, turned, tiles,
                e_own, e_all, tc_sem, coef_sem, eps_sem,
                g_send, g_recv, c_send, c_recv, z_send, z_recv, t_send, t_recv, e_send, e_recv):
    me = lax.axis_index("aux")
    blk = lax.axis_index("blk")
    nz = nb // 2
    core = lax.rem(blk, 2)
    zed = lax.div(blk, 2)
    vir = eps_ref.shape[1]
    rows = vir // nb
    span = tc_buf.shape[3]
    depth = tc_buf.shape[2]
    ring = na == 4

    def blk_peer(d):
        return (me, lax.rem(blk + d, nb))

    def z_peer(d):
        return (me, 2 * lax.rem(zed + d, nz) + core)

    if ring:
        after = (lax.rem(me, 2) * 2 + 1 - lax.div(me, 2), blk)
        before = ((1 - lax.rem(me, 2)) * 2 + lax.div(me, 2), blk)
        aux_peers = [after, before]
    else:
        aux_peers = [(lax.rem(me + d, na), blk) for d in range(1, na)]
    barrier = pltpu.get_barrier_semaphore()
    for peer in aux_peers + [blk_peer(d) for d in range(1, nb)]:
        pl.semaphore_signal(barrier, inc=1, device_id=peer, device_id_type=MESH)

    loads = []
    chunks = coef_sem.shape[0]
    per_chunk = coef_buf.shape[0] // chunks
    for n in range(chunks):
        part_of = pl.ds(n * per_chunk, per_chunk)
        loads.append(pltpu.make_async_copy(coef_hbm.at[part_of], coef_buf.at[part_of], coef_sem.at[n]))
    tc_loads = [pltpu.make_async_copy(tc_hbm.at[s], tc_buf.at[s], tc_sem.at[s]) for s in range(slots)]
    eps_load = pltpu.make_async_copy(eps_hbm, eps_buf, eps_sem)
    for c in loads + tc_loads + [eps_load]:
        c.start()
    for c in loads:
        c.wait()
    for s in range(slots):
        block = coef_buf[block_ref[s]]
        for k in range(AUX_BLOCKS_DEV):
            used = jnp.logical_and(s < live_ref[0], aux_ref[s] == k)
            scale = jnp.where(used, 1.0, 0.0).astype(jnp.float32)
            weights[s * span:(s + 1) * span, k * vir:(k + 1) * vir] = (
                block.astype(jnp.float32) * scale).astype(jnp.bfloat16)
    for c in tc_loads:
        c.wait()

    def transform(i):
        left = jnp.concatenate([tc_buf[s, i] for s in range(slots)], axis=1)
        res = jnp.dot(left, weights[...], preferred_element_type=jnp.float32)
        for k in range(AUX_BLOCKS_DEV):
            half[i, k * depth:(k + 1) * depth, :] = res[:, k * vir:(k + 1) * vir].astype(jnp.bfloat16)

    def remote(src, slot, j, peer):
        return pltpu.make_async_remote_copy(
            src_ref=src, dst_ref=held.at[slot, j], send_sem=g_send.at[slot, j], recv_sem=g_recv.at[slot, j],
            device_id=peer, device_id_type=MESH)

    def add(src, first):
        left = jnp.transpose(src[me])
        for j in range(na):
            cols = slice(j * vir, (j + 1) * vir)
            res = jnp.dot(left, src[j], preferred_element_type=jnp.float32)
            for k in range(nb):
                piece = res[k * rows:(k + 1) * rows]
                if first:
                    part[k % 2, k // 2, :, cols] = piece
                else:
                    part[k % 2, k // 2, :, cols] += piece

    gathers = []
    if ring:
        to_after = [remote(half.at[j], 0, j, after) for j in range(na)]
        to_before = [remote(half.at[j], 2, j, before) for j in range(na)]
        transform(0)
        pl.semaphore_wait(barrier, len(aux_peers) + nb - 1)
        to_after[0].start()
        transform(2)
        to_before[2].start()
        transform(1)
        to_after[1].start()
        transform(3)
        to_before[3].start()
        for j in (2, 3):
            to_after[j].start()
        for j in (0, 1):
            to_before[j].start()
        passed = [remote(held.at[0, j], 1, j, after) for j in (0, 1)]
        passed += [remote(held.at[2, j], 1, j, before) for j in (2, 3)]
        for early, late in ((0, 2), (1, 3)):
            to_after[early].wait_recv()
            passed[early].start()
            to_before[late].wait_recv()
            passed[late].start()
        add(half, True)
        for j in (2, 3):
            to_after[j].wait_recv()
        add(held.at[0], False)
        for j in (0, 1):
            to_before[j].wait_recv()
        add(held.at[2], False)
        for c in passed:
            c.wait_recv()
        add(held.at[1], False)
        gathers = to_after + to_before + passed
    else:
        for j in range(na):
            transform(j)
        pl.semaphore_wait(barrier, len(aux_peers) + nb - 1)
        for d in range(1, na):
            for j in range(na):
                gathers.append(remote(half.at[j], d - 1, j, aux_peers[d - 1]))
                gathers[-1].start()
        add(half, True)
        for d in range(1, na):
            for j in range(na):
                gathers[(d - 1) * na + j].wait_recv()
            add(held.at[d - 1], False)
    eps_load.wait()

    swap = pltpu.make_async_remote_copy(
        src_ref=part.at[1 - core], dst_ref=core_in, send_sem=c_send, recv_sem=c_recv,
        device_id=(me, 2 * zed + 1 - core), device_id_type=MESH)
    swap.start()
    swap.wait_recv()
    sends = []
    for d in range(1, nz):
        to = lax.rem(zed + d, nz)
        out_z[d - 1] = (part[core, to] + core_in[to]).astype(jnp.bfloat16)
        sends.append(pltpu.make_async_remote_copy(
            src_ref=out_z.at[d - 1], dst_ref=in_z.at[d - 1], send_sem=z_send.at[d - 1],
            recv_sem=z_recv.at[d - 1], device_id=z_peer(d), device_id_type=MESH))
        sends[-1].start()
    total = part[core, zed] + core_in[zed]
    for d in range(1, nz):
        sends[d - 1].wait_recv()
        total = total + in_z[d - 1].astype(jnp.float32)

    pieces = [total[:, j * vir:(j + 1) * vir] for j in range(na)]
    stacked = pieces
    if na * rows < LANES:
        stacked = pieces + [jnp.zeros((LANES - na * rows, vir), jnp.float32)]
    turned[...] = jnp.transpose(jnp.concatenate(stacked, axis=0))
    swaps = []
    for d in range(1, nb):
        to = lax.rem(blk + d, nb)
        swaps.append(pltpu.make_async_remote_copy(
            src_ref=turned.at[pl.ds(pl.multiple_of(to * rows, rows), rows)], dst_ref=tiles.at[blk],
            send_sem=t_send.at[d - 1], recv_sem=t_recv.at[d - 1],
            device_id=blk_peer(d), device_id_type=MESH))
        swaps[-1].start()
    tiles[blk] = turned[pl.ds(pl.multiple_of(blk * rows, rows), rows), :]

    level = eps_ref[...]
    turn = jnp.transpose(jnp.broadcast_to(level, (LANES, vir)))
    own_level = eps_buf[index_ref[me]]
    column = jnp.zeros((rows, LANES), jnp.float32)
    for k in range(nb):
        column = jnp.where(blk == k, turn[k * rows:(k + 1) * rows], column)
    column = column[:, :1]
    ratios = []
    for j in range(na):
        ratio = pieces[j] / (((own_level + eps_buf[index_ref[j]]) - column) - level)
        amp_ref[0, :, j, :] = ratio
        ratios.append(ratio)

    for c in swaps:
        c.wait_recv()
    lane = lax.broadcasted_iota(jnp.int32, (rows, LANES), 1)
    lane_e = lax.broadcasted_iota(jnp.int32, (8, LANES), 1)
    per = LANES // rows
    energy = jnp.zeros((8, LANES), jnp.float32)
    for j in range(na):
        groups = []
        for g in range(vir // LANES):
            crossed = jnp.zeros((rows, LANES), jnp.float32)
            for m in range(per):
                tile = tiles[g * per + m]
                shift = (rows * (m - j)) % LANES
                if shift:
                    tile = pltpu.roll(tile, shift, 1)
                crossed = jnp.where(lax.div(lane, rows) == m, tile, crossed)
            groups.append(crossed)
        crossed = jnp.concatenate(groups, axis=1)
        value = jnp.sum(ratios[j] * (2.0 * pieces[j] - crossed))
        energy = jnp.where(lane_e == j, value, energy)
    e_own[...] = energy
    e_all[blk] = energy
    e_sends = []
    for d in range(1, nb):
        e_sends.append(pltpu.make_async_remote_copy(
            src_ref=e_own, dst_ref=e_all.at[blk], send_sem=e_send.at[d - 1], recv_sem=e_recv.at[d - 1],
            device_id=blk_peer(d), device_id_type=MESH))
        e_sends[-1].start()
    for c in e_sends:
        c.wait_recv()
    result = e_all[0]
    for k in range(1, nb):
        result = result + e_all[k]
    e_ref[...] = result[:1, :na]
    for c in gathers + [swap] + sends + swaps + e_sends:
        c.wait_send()


def body(three_center, slot_block, slot_aux, live_slots, vir_coef, eps_occ, eps_vir, occ_index):
    na = lax.axis_size("aux")
    nb = lax.axis_size("blk")
    nz = nb // 2
    slots, occ, aux_rows, span = three_center.shape
    vir = vir_coef.shape[1]
    depth = AUX_BLOCKS_DEV * aux_rows
    wide = occ * vir
    rows = vir // nb
    smem = pl.BlockSpec(memory_space=pltpu.SMEM)
    vmem = pl.BlockSpec(memory_space=pltpu.VMEM)
    anyspace = pl.BlockSpec(memory_space=pl.ANY)
    blocks = vir_coef.shape[0] // span
    chunks = max(n for n in range(1, 9) if blocks % n == 0)
    dma = pltpu.SemaphoreType.DMA
    return pl.pallas_call(
        functools.partial(pair_kernel, na, nb, slots),
        out_shape=(jax.ShapeDtypeStruct((1, rows, occ, vir), jnp.float32),
                   jax.ShapeDtypeStruct((1, na), jnp.float32)),
        in_specs=[smem] * 4 + [anyspace] * 3 + [vmem],
        out_specs=(vmem, vmem),
        scratch_shapes=[
            pltpu.VMEM((slots, occ, aux_rows, span), jnp.bfloat16),
            pltpu.VMEM((blocks, span, vir), jnp.bfloat16),
            pltpu.VMEM((slots * span, AUX_BLOCKS_DEV * vir), jnp.bfloat16),
            pltpu.SMEM((eps_occ.shape[0],), jnp.float32),
            pltpu.VMEM((occ, depth, vir), jnp.bfloat16),
            pltpu.VMEM((na - 1, occ, depth, vir), jnp.bfloat16),
            pltpu.VMEM((2, nz, rows, wide), jnp.float32),
            pltpu.VMEM((nz, rows, wide), jnp.float32),
            pltpu.VMEM((nz - 1, rows, wide), jnp.bfloat16),
            pltpu.VMEM((nz - 1, rows, wide), jnp.bfloat16),
            pltpu.VMEM((vir, LANES), jnp.float32),
            pltpu.VMEM((nb, rows, LANES), jnp.float32),
            pltpu.VMEM((8, LANES), jnp.float32),
            pltpu.VMEM((nb, 8, LANES), jnp.float32),
            dma((slots,)), dma((chunks,)), dma,
            dma((na - 1, na)), dma((na - 1, na)), dma, dma, dma((nz - 1,)), dma((nz - 1,)),
            dma((nb - 1,)), dma((nb - 1,)), dma((nb - 1,)), dma((nb - 1,)),
        ],
        compiler_params=pltpu.CompilerParams(collective_id=0, has_side_effects=True),
    )(slot_block, slot_aux, live_slots, occ_index, three_center,
      vir_coef.reshape(blocks, span, vir), eps_occ, eps_vir.reshape(1, vir))


def solution(mesh):
    in_specs = (
        P(("aux", "blk"), None, None, None),
        P(("aux", "blk")),
        P(("aux", "blk")),
        P(("aux", "blk")),
        P(),
        P(),
        P(),
        P(),
    )
    out_specs = (P("aux", "blk", None, None), P("aux", None))
    return jax.shard_map(body, mesh=mesh, in_specs=in_specs, out_specs=out_specs, check_vma=False)
```

time: 57.5 us -> 48.6 us (0.85)
  Pallas kernels: 53.1 us -> 44.4 us
    pallas_call x2 -> x1, Pallas kernels: 53.1 us -> 44.4 us  [body(): pl.pallas_call(functools.partial(pair_kernel, na, nb, slots), out_shape=(...]
    reshape x1 -> x0, local copies, waits for them, and re-layouts: 1.62 us -> none  [body(): return (amp.reshape(1, rows, occ, vir), energy)]
    unnamed x1 -> x2, local copies, waits for them, and re-layouts: 1.14 us -> 2.74 us
where the time goes in v2:
time: 48.6 us; the launch traced here: 48.4 us
  Pallas kernels  44.4 us (91%)
  local copies, waits for them, and re-layouts  2.74 us (6%)
  between operations  1.29 us (3%)
    pallas_call x1, Pallas kernels, body(): pl.pallas_call(functools.partial(pair_kernel, na, nb, slots), out_shape=(...  44.4 us
    unnamed x2, local copies, waits for them, and re-layouts  2.74 us

profile of v2, /device:TPU:0, one launch (start us, length us, event | category | flops | bytes accessed | tf_op | source)
XLA Modules:
  0.0 48.4 jit_solution(13457005929586287325)
XLA Ops:
  1.3 44.4 %shard_map.95 = (f32[1,32,4,256]{3,2,1,0:T(4,128)}, f32[1,4]{1,0:T(1,128)}) custom-call(s32[12]{0:T(128)} %block_ref.1, s32[12]{0:T(128)} %aux_ref.1, s32[1]{0:T(128)S(6)} %copy.12.live_ref, s32[4]{0:T(128)} %index_ref.1, bf16[12,4,128,128]{3,2,1,0:T(8,128)(2,1)} %tc_hbm.1, bf16[48,128,256]{2,1,0:T(8,128)(2,1)} %bitcast.2, f32[4000]{0:T(1024)} %eps_hbm.1, ...), custom_call_target="tpu_custom_call" | custom-call | tf_op jit(solution)/shard_map/pallas_call | solution.py:241
  45.6 1.6 %copy.13 = f32[1,32,4,256]{3,2,1,0:T(4,128)} copy(f32[1,32,4,256]{3,2,1,0:T(4,128)} %get-tuple-element.4) | data formatting | bytes 262144
  47.2 1.2 %copy.14 = f32[1,4]{1,0:T(1,128)} copy(f32[1,4]{1,0:T(1,128)} %get-tuple-element.5) | data formatting | bytes 32

commit v3 on v2

v3 whole, which is shorter than its diff:
```python
import functools

import jax
import jax.numpy as jnp
from jax import lax
from jax.experimental import pallas as pl
from jax.experimental.pallas import tpu as pltpu
from jax.sharding import PartitionSpec as P

AUX_BLOCKS_DEV = 2
MESH = pl.DeviceIdType.MESH
LANES = 128


def pair_kernel(na, nb, slots, block_ref, aux_ref, live_ref, index_ref, tc_hbm, coef_hbm, eps_hbm, eps_ref,
                amp_ref, e_ref,
                tc_buf, coef_buf, weights, eps_buf, half, held, part, core_in, out_z, in_z, turned, tiles,
                packs, tail, e_own, e_all, e_tail, tc_sem, coef_sem, eps_sem,
                g_send, g_recv, c_send, c_recv, z_send, z_recv, t_send, t_recv, n_send, n_recv,
                e_send, e_recv, f_send, f_recv):
    me = lax.axis_index("aux")
    blk = lax.axis_index("blk")
    nz = nb // 2
    core = lax.rem(blk, 2)
    zed = lax.div(blk, 2)
    vir = eps_ref.shape[1]
    rows = vir // nb
    span = tc_buf.shape[3]
    depth = tc_buf.shape[2]
    ring = na == 4
    kept = na // 2 + 1
    rest = na - kept

    def gray(x):
        return lax.div(x, 2) * 2 + lax.rem(lax.rem(x, 2) + lax.div(x, 2), 2)

    def at(t):
        if ring:
            return gray(lax.rem(gray(me) + t % na, na))
        return lax.rem(me + t % na, na)

    def blk_peer(d):
        return (me, lax.rem(blk + d, nb))

    def z_peer(d):
        return (me, 2 * lax.rem(zed + d, nz) + core)

    steps = (1, na - 1) if ring else tuple(range(1, na))
    barrier = pltpu.get_barrier_semaphore()
    sources = [(at(-d), blk) for d in steps] + [blk_peer(d) for d in range(1, nb)]
    for u in range(1, rest + 1):
        sources += [(at(-u), lax.rem(blk + d, nb)) for d in range(1, nb)]
    for peer in sources:
        pl.semaphore_signal(barrier, inc=1, device_id=peer, device_id_type=MESH)

    loads = []
    chunks = coef_sem.shape[0]
    per_chunk = coef_buf.shape[0] // chunks
    for n in range(chunks):
        part_of = pl.ds(n * per_chunk, per_chunk)
        loads.append(pltpu.make_async_copy(coef_hbm.at[part_of], coef_buf.at[part_of], coef_sem.at[n]))
    tc_loads = [pltpu.make_async_copy(tc_hbm.at[s], tc_buf.at[s], tc_sem.at[s]) for s in range(slots)]
    eps_load = pltpu.make_async_copy(eps_hbm, eps_buf, eps_sem)
    for c in loads + tc_loads + [eps_load]:
        c.start()
    for c in loads:
        c.wait()
    for s in range(slots):
        block = coef_buf[block_ref[s]]
        for k in range(AUX_BLOCKS_DEV):
            used = jnp.logical_and(s < live_ref[0], aux_ref[s] == k)
            scale = jnp.where(used, 1.0, 0.0).astype(jnp.float32)
            weights[s * span:(s + 1) * span, k * vir:(k + 1) * vir] = (
                block.astype(jnp.float32) * scale).astype(jnp.bfloat16)
    for c in tc_loads:
        c.wait()

    def transform(i):
        left = jnp.concatenate([tc_buf[s, i] for s in range(slots)], axis=1)
        res = jnp.dot(left, weights[...], preferred_element_type=jnp.float32)
        for k in range(AUX_BLOCKS_DEV):
            half[i, k * depth:(k + 1) * depth, :] = res[:, k * vir:(k + 1) * vir].astype(jnp.bfloat16)

    def remote(src, dst, slot, n, peer):
        return pltpu.make_async_remote_copy(
            src_ref=src, dst_ref=dst, send_sem=g_send.at[slot, n], recv_sem=g_recv.at[slot, n],
            device_id=peer, device_id_type=MESH)

    def add(block, first):
        left = jnp.transpose(block(0))
        for t in range(kept):
            cols = slice(t * vir, (t + 1) * vir)
            res = jnp.dot(left, block(t), preferred_element_type=jnp.float32)
            for k in range(nb):
                piece = res[k * rows:(k + 1) * rows]
                if first:
                    part[k % 2, k // 2, :, cols] = piece
                else:
                    part[k % 2, k // 2, :, cols] += piece

    for i in range(na):
        transform(i)
    pl.semaphore_wait(barrier, len(sources))
    if ring:
        after, before = (at(1), blk), (at(-1), blk)
        mid = AUX_BLOCKS_DEV * depth // 2
        low, high = pl.ds(0, mid), pl.ds(mid, mid)
        to_after = [remote(half.at[at(1 + t)], held.at[0, t], 0, t, after) for t in range(kept)]
        to_before = [remote(half.at[at(t - 1)], held.at[2, t], 2, t, before) for t in range(kept)]
        for c in (to_after[1], to_before[1], to_after[2], to_before[0], to_after[0], to_before[2]):
            c.start()
        passed = [
            remote(held.at[0, 1], held.at[1, 0], 1, 0, after),
            remote(held.at[0, 2, low], held.at[1, 1, low], 1, 1, after),
            remote(held.at[2, 1], held.at[1, 2], 1, 2, before),
            remote(held.at[2, 0, high], held.at[1, 1, high], 1, 3, before),
        ]
        for got, on in ((to_after[1], 0), (to_before[1], 2), (to_after[2], 1), (to_before[0], 3)):
            got.wait_recv()
            passed[on].start()
        add(lambda t: half[at(t)], True)
        to_after[0].wait_recv()
        add(lambda t: held[0, t], False)
        to_before[2].wait_recv()
        add(lambda t: held[2, t], False)
        for c in passed:
            c.wait_recv()
        add(lambda t: held[1, t], False)
        gathers = to_after + to_before + passed
    else:
        gathers = []
        for d in range(1, na):
            for t in range(kept):
                gathers.append(remote(half.at[at(d + t)], held.at[d - 1, t], d - 1, t, (at(d), blk)))
                gathers[-1].start()
        add(lambda t: half[at(t)], True)
        for d in range(1, na):
            for t in range(kept):
                gathers[(d - 1) * kept + t].wait_recv()
            add(lambda t: held[d - 1, t], False)
    eps_load.wait()

    swap = pltpu.make_async_remote_copy(
        src_ref=part.at[1 - core], dst_ref=core_in, send_sem=c_send, recv_sem=c_recv,
        device_id=(me, 2 * zed + 1 - core), device_id_type=MESH)
    swap.start()
    swap.wait_recv()
    sends = []
    for d in range(1, nz):
        to = lax.rem(zed + d, nz)
        out_z[d - 1] = (part[core, to] + core_in[to]).astype(jnp.bfloat16)
        sends.append(pltpu.make_async_remote_copy(
            src_ref=out_z.at[d - 1], dst_ref=in_z.at[d - 1], send_sem=z_send.at[d - 1],
            recv_sem=z_recv.at[d - 1], device_id=z_peer(d), device_id_type=MESH))
        sends[-1].start()
    total = part[core, zed] + core_in[zed]
    for d in range(1, nz):
        sends[d - 1].wait_recv()
        total = total + in_z[d - 1].astype(jnp.float32)

    pieces = [total[:, t * vir:(t + 1) * vir] for t in range(kept)]
    stacked = pieces
    if kept * rows < LANES:
        stacked = pieces + [jnp.zeros((LANES - kept * rows, vir), jnp.float32)]
    flat = jnp.transpose(jnp.concatenate(stacked, axis=0))
    turned[...] = flat
    lane = lax.broadcasted_iota(jnp.int32, (rows, LANES), 1)
    lane_e = lax.broadcasted_iota(jnp.int32, (8, LANES), 1)
    per = LANES // rows
    bands = rows // 8

    def rolled(value, shift):
        shift = shift % LANES
        return pltpu.roll(value, shift, 1) if shift else value

    for u in range(1, rest + 1):
        for k in range(nb):
            packed = jnp.zeros((8, LANES), jnp.float32)
            for q in range(bands):
                band = flat[k * rows + 8 * q:k * rows + 8 * q + 8]
                packed = jnp.where(lax.div(lane_e, rows) == q, rolled(band, rows * (q - u)), packed)
            packs[u - 1, k] = packed
    tails = []
    for u in range(1, rest + 1):
        for d in range(nb):
            to = lax.rem(blk + d, nb)
            tails.append(pltpu.make_async_remote_copy(
                src_ref=packs.at[u - 1, to], dst_ref=tail.at[u - 1, blk],
                send_sem=n_send.at[u - 1, d], recv_sem=n_recv.at[u - 1, d],
                device_id=(at(u), to), device_id_type=MESH))
            tails[-1].start()
    swaps = []
    for d in range(1, nb):
        to = lax.rem(blk + d, nb)
        swaps.append(pltpu.make_async_remote_copy(
            src_ref=turned.at[pl.ds(pl.multiple_of(to * rows, rows), rows)], dst_ref=tiles.at[blk],
            send_sem=t_send.at[d - 1], recv_sem=t_recv.at[d - 1],
            device_id=blk_peer(d), device_id_type=MESH))
        swaps[-1].start()
    tiles[blk] = turned[pl.ds(pl.multiple_of(blk * rows, rows), rows), :]

    level = eps_ref[...]
    turn = jnp.transpose(jnp.broadcast_to(level, (LANES, vir)))
    own_level = eps_buf[index_ref[me]]
    column = jnp.zeros((rows, LANES), jnp.float32)
    for k in range(nb):
        column = jnp.where(blk == k, turn[k * rows:(k + 1) * rows], column)
    column = column[:, :1]
    def ratio_of(t, piece):
        return piece / (((own_level + eps_buf[index_ref[at(t)]]) - column) - level)

    ratios = [ratio_of(t, pieces[t]) for t in range(kept)]
    scores = [ratios[t] * pieces[t] * 2.0 for t in range(kept)]
    for c in swaps:
        c.wait_recv()
    energy = jnp.zeros((8, LANES), jnp.float32)
    for t in range(kept):
        groups = []
        for g in range(vir // LANES):
            crossed = jnp.zeros((rows, LANES), jnp.float32)
            for m in range(per):
                crossed = jnp.where(lax.div(lane, rows) == m, rolled(tiles[g * per + m], rows * (m - t)), crossed)
            groups.append(crossed)
        crossed = jnp.concatenate(groups, axis=1)
        value = jnp.sum(scores[t] - ratios[t] * crossed)
        energy = jnp.where(lane_e == t, value, energy)
    e_own[...] = energy
    e_all[blk] = energy
    e_sends = []
    for d in range(1, nb):
        e_sends.append(pltpu.make_async_remote_copy(
            src_ref=e_own, dst_ref=e_all.at[blk], send_sem=e_send.at[d - 1], recv_sem=e_recv.at[d - 1],
            device_id=blk_peer(d), device_id_type=MESH))
        e_sends[-1].start()
    for u in range(1, rest + 1):
        for d in range(nb):
            e_sends.append(pltpu.make_async_remote_copy(
                src_ref=e_own, dst_ref=e_tail.at[u - 1, blk],
                send_sem=f_send.at[u - 1, d], recv_sem=f_recv.at[u - 1, d],
                device_id=(at(u), lax.rem(blk + d, nb)), device_id_type=MESH))
            e_sends[-1].start()

    for c in tails:
        c.wait_recv()
    for u in range(rest, 0, -1):
        groups = []
        for g in range(vir // LANES):
            strips = []
            for q in range(bands):
                strip = jnp.zeros((8, LANES), jnp.float32)
                for m in range(per):
                    moved = rolled(tail[u - 1, g * per + m], rows * (m - q))
                    strip = jnp.where(lax.div(lane_e, rows) == m, moved, strip)
                strips.append(strip)
            groups.append(jnp.concatenate(strips, axis=0))
        ratios.append(ratio_of(na - u, jnp.concatenate(groups, axis=1)))
    for j in range(na):
        chosen = ratios[0]
        for t in range(1, na):
            chosen = jnp.where(at(t) == j, ratios[t], chosen)
        amp_ref[0, :, j, :] = chosen

    for c in e_sends:
        c.wait_recv()
    sums = [e_all[...]] + [e_tail[u - 1] for u in range(1, rest + 1)]
    totals = []
    for group in sums:
        result = group[0]
        for k in range(1, nb):
            result = result + group[k]
        totals.append(result)
    final = jnp.zeros((8, LANES), jnp.float32)
    for t in range(na):
        group, place = (totals[0], t) if t < kept else (totals[na - t], na - t)
        value = jnp.sum(jnp.where(lane_e == place, group, 0.0)[:1], axis=1, keepdims=True)
        final = jnp.where(lane_e == at(t), value, final)
    e_ref[...] = final[:1, :na]
    for c in gathers + [swap] + sends + swaps + tails + e_sends:
        c.wait_send()


def body(three_center, slot_block, slot_aux, live_slots, vir_coef, eps_occ, eps_vir, occ_index):
    na = lax.axis_size("aux")
    nb = lax.axis_size("blk")
    nz = nb // 2
    slots, occ, aux_rows, span = three_center.shape
    vir = vir_coef.shape[1]
    depth = AUX_BLOCKS_DEV * aux_rows
    kept = na // 2 + 1
    rest = na - kept
    wide = kept * vir
    rows = vir // nb
    smem = pl.BlockSpec(memory_space=pltpu.SMEM)
    vmem = pl.BlockSpec(memory_space=pltpu.VMEM)
    anyspace = pl.BlockSpec(memory_space=pl.ANY)
    blocks = vir_coef.shape[0] // span
    chunks = max(n for n in range(1, 9) if blocks % n == 0)
    dma = pltpu.SemaphoreType.DMA
    return pl.pallas_call(
        functools.partial(pair_kernel, na, nb, slots),
        out_shape=(jax.ShapeDtypeStruct((1, rows, occ, vir), jnp.float32),
                   jax.ShapeDtypeStruct((1, na), jnp.float32)),
        in_specs=[smem] * 4 + [anyspace] * 3 + [vmem],
        out_specs=(vmem, vmem),
        scratch_shapes=[
            pltpu.VMEM((slots, occ, aux_rows, span), jnp.bfloat16),
            pltpu.VMEM((blocks, span, vir), jnp.bfloat16),
            pltpu.VMEM((slots * span, AUX_BLOCKS_DEV * vir), jnp.bfloat16),
            pltpu.SMEM((eps_occ.shape[0],), jnp.float32),
            pltpu.VMEM((occ, depth, vir), jnp.bfloat16),
            pltpu.VMEM((na - 1, kept, depth, vir), jnp.bfloat16),
            pltpu.VMEM((2, nz, rows, wide), jnp.float32),
            pltpu.VMEM((nz, rows, wide), jnp.float32),
            pltpu.VMEM((nz - 1, rows, wide), jnp.bfloat16),
            pltpu.VMEM((nz - 1, rows, wide), jnp.bfloat16),
            pltpu.VMEM((vir, LANES), jnp.float32),
            pltpu.VMEM((nb, rows, LANES), jnp.float32),
            pltpu.VMEM((rest, nb, 8, LANES), jnp.float32),
            pltpu.VMEM((rest, nb, 8, LANES), jnp.float32),
            pltpu.VMEM((8, LANES), jnp.float32),
            pltpu.VMEM((nb, 8, LANES), jnp.float32),
            pltpu.VMEM((rest, nb, 8, LANES), jnp.float32),
            dma((slots,)), dma((chunks,)), dma,
            dma((na - 1, kept + 1)), dma((na - 1, kept + 1)), dma, dma, dma((nz - 1,)), dma((nz - 1,)),
            dma((nb - 1,)), dma((nb - 1,)), dma((rest, nb)), dma((rest, nb)),
            dma((nb - 1,)), dma((nb - 1,)), dma((rest, nb)), dma((rest, nb)),
        ],
        compiler_params=pltpu.CompilerParams(collective_id=0, has_side_effects=True),
    )(slot_block, slot_aux, live_slots, occ_index, three_center,
      vir_coef.reshape(blocks, span, vir), eps_occ, eps_vir.reshape(1, vir))


def solution(mesh):
    in_specs = (
        P(("aux", "blk"), None, None, None),
        P(("aux", "blk")),
        P(("aux", "blk")),
        P(("aux", "blk")),
        P(),
        P(),
        P(),
        P(),
    )
    out_specs = (P("aux", "blk", None, None), P("aux", None))
    return jax.shard_map(body, mesh=mesh, in_specs=in_specs, out_specs=out_specs, check_vma=False)
```

time: 48.6 us -> 45.6 us (0.938)
  Pallas kernels: 44.4 us -> 41.4 us
    pallas_call x1, Pallas kernels: 44.4 us -> 41.4 us  [body(): pl.pallas_call(functools.partial(pair_kernel, na, nb, slots), out_shape=(...]
where the time goes in v3:
time: 45.6 us; the launch traced here: 45.5 us
  Pallas kernels  41.4 us (91%)
  local copies, waits for them, and re-layouts  2.74 us (6%)
  between operations  1.29 us (3%)
    pallas_call x1, Pallas kernels, body(): pl.pallas_call(functools.partial(pair_kernel, na, nb, slots), out_shape=(...  41.4 us
    unnamed x2, local copies, waits for them, and re-layouts  2.74 us

profile of v3, /device:TPU:0, one launch (start us, length us, event | category | flops | bytes accessed | tf_op | source)
XLA Modules:
  0.0 45.5 jit_solution(17327870790191148136)
XLA Ops:
  1.3 41.4 %shard_map.95 = (f32[1,32,4,256]{3,2,1,0:T(4,128)}, f32[1,4]{1,0:T(1,128)}) custom-call(s32[12]{0:T(128)} %block_ref.1, s32[12]{0:T(128)} %aux_ref.1, s32[1]{0:T(128)S(6)} %copy.12.live_ref, s32[4]{0:T(128)} %index_ref.1, bf16[12,4,128,128]{3,2,1,0:T(8,128)(2,1)} %tc_hbm.1, bf16[48,128,256]{2,1,0:T(8,128)(2,1)} %bitcast.2, f32[4000]{0:T(1024)} %eps_hbm.1, ...), custom_call_target="tpu_custom_call" | custom-call | tf_op jit(solution)/shard_map/pallas_call | solution.py:299
  42.7 1.6 %copy.13 = f32[1,32,4,256]{3,2,1,0:T(4,128)} copy(f32[1,32,4,256]{3,2,1,0:T(4,128)} %get-tuple-element.4) | data formatting | bytes 262144
  44.3 1.2 %copy.14 = f32[1,4]{1,0:T(1,128)} copy(f32[1,4]{1,0:T(1,128)} %get-tuple-element.5) | data formatting | bytes 32

commit v4 on v3

--- a/solution.py
+++ b/solution.py
@@ -292,7 +292,7 @@
     rows = vir // nb
     smem = pl.BlockSpec(memory_space=pltpu.SMEM)
     vmem = pl.BlockSpec(memory_space=pltpu.VMEM)
-    anyspace = pl.BlockSpec(memory_space=pl.ANY)
+    anyspace = pl.BlockSpec(memory_space=pltpu.HBM)
     blocks = vir_coef.shape[0] // span
     chunks = max(n for n in range(1, 9) if blocks % n == 0)
     dma = pltpu.SemaphoreType.DMA
@@ -325,7 +325,7 @@
             dma((nb - 1,)), dma((nb - 1,)), dma((rest, nb)), dma((rest, nb)),
             dma((nb - 1,)), dma((nb - 1,)), dma((rest, nb)), dma((rest, nb)),
         ],
-        compiler_params=pltpu.CompilerParams(collective_id=0, has_side_effects=True),
+        compiler_params=pltpu.CompilerParams(collective_id=0, has_side_effects=True, vmem_limit_bytes=56000000),
     )(slot_block, slot_aux, live_slots, occ_index, three_center,
       vir_coef.reshape(blocks, span, vir), eps_occ, eps_vir.reshape(1, vir))
 

time: 45.6 us -> 46.7 us (1.024)
  local copies, waits for them, and re-layouts: 2.74 us -> 4.52 us
  Pallas kernels: 41.4 us -> 40.6 us
    unnamed x2 -> x12, local copies, waits for them, and re-layouts: 2.74 us -> 4.52 us
    pallas_call x1, Pallas kernels: 41.4 us -> 40.6 us  [body(): pl.pallas_call(functools.partial(pair_kernel, na, nb, slots), out_shape=(...]
where the time goes in v4:
time: 46.7 us; the launch traced here: 46.4 us
  Pallas kernels  40.6 us (87%)
  local copies, waits for them, and re-layouts  4.52 us (10%)
  between operations  1.3 us (3%)
    pallas_call x1, Pallas kernels, body(): pl.pallas_call(functools.partial(pair_kernel, na, nb, slots), out_shape=(...  40.6 us
    unnamed x12, local copies, waits for them, and re-layouts  4.52 us

profile of v4, /device:TPU:0, one launch (start us, length us, event | category | flops | bytes accessed | tf_op | source)
XLA Modules:
  0.0 46.4 jit_solution(1095769528621496295)
XLA Ops:
  1.3 0.0 copy-start
  1.3 0.7 %copy-done = f32[4000]{0:T(1024)S(1)} copy-done((f32[4000]{0:T(1024)S(1)}, f32[4000]{0:T(1024)}, u32[]{:S(2)}) %copy-start) | copy-done | bytes 16024
  2.0 0.0 copy-start.1
  2.0 0.7 %copy-done.1 = f32[256]{0:T(256)S(1)} copy-done((f32[256]{0:T(256)S(1)}, f32[256]{0:T(256)}, u32[]{:S(2)}) %copy-start.1) | copy-done | bytes 1048
  2.7 0.0 copy-start.2
  2.7 0.7 %copy-done.2 = s32[12]{0:T(128)S(1)} copy-done((s32[12]{0:T(128)S(1)}, s32[12]{0:T(128)}, u32[]{:S(2)}) %copy-start.2) | copy-done | bytes 72
  3.3 0.0 copy-start.3
  3.3 0.7 %copy-done.3 = s32[12]{0:T(128)S(1)} copy-done((s32[12]{0:T(128)S(1)}, s32[12]{0:T(128)}, u32[]{:S(2)}) %copy-start.3) | copy-done | bytes 72
  4.0 0.0 copy-start.4
  4.0 0.7 %copy-done.4 = s32[4]{0:T(128)S(1)} copy-done((s32[4]{0:T(128)S(1)}, s32[4]{0:T(128)}, u32[]{:S(2)}) %copy-start.4) | copy-done | bytes 40
  4.6 40.6 %shard_map.95 = (f32[1,32,4,256]{3,2,1,0:T(4,128)S(1)}, f32[1,4]{1,0:T(1,128)S(1)}) custom-call(s32[12]{0:T(128)S(1)} %copy-done.2, s32[12]{0:T(128)S(1)} %copy-done.3, s32[1]{0:T(128)S(6)} %copy.12.live_ref, s32[4]{0:T(128)S(1)} %copy-done.4, bf16[12,4,128,128]{3,2,1,0:T(8,128)(2,1)} %tc_hbm.1, bf16[48,128,256]{2,1,0:T(8,128)(2,1)} %bitcast.3, ...), custom_call_target="tpu_custom_call" | custom-call | tf_op jit(solution)/shard_map/pallas_call | solution.py:299
  45.3 0.7 %copy.13 = f32[1,32,4,256]{3,2,1,0:T(4,128)} copy(f32[1,32,4,256]{3,2,1,0:T(4,128)S(1)} %get-tuple-element.4) | data formatting | bytes 262144
  45.9 0.5 %copy.14 = f32[1,4]{1,0:T(1,128)} copy(f32[1,4]{1,0:T(1,128)S(1)} %get-tuple-element.5) | data formatting | bytes 32
Async XLA Ops:
  1.3 0.7 %copy-start = (f32[4000]{0:T(1024)S(1)}, f32[4000]{0:T(1024)}, u32[]{:S(2)}) copy-start(f32[4000]{0:T(1024)} %eps_hbm.1) | copy-start | bytes 48004
  2.0 0.7 %copy-start.1 = (f32[256]{0:T(256)S(1)}, f32[256]{0:T(256)}, u32[]{:S(2)}) copy-start(f32[256]{0:T(256)} %param.14) | copy-start | bytes 3076
  2.7 0.7 %copy-start.2 = (s32[12]{0:T(128)S(1)}, s32[12]{0:T(128)}, u32[]{:S(2)}) copy-start(s32[12]{0:T(128)} %block_ref.1) | copy-start | bytes 148
  3.3 0.7 %copy-start.3 = (s32[12]{0:T(128)S(1)}, s32[12]{0:T(128)}, u32[]{:S(2)}) copy-start(s32[12]{0:T(128)} %aux_ref.1) | copy-start | bytes 148
  4.0 0.7 %copy-start.4 = (s32[4]{0:T(128)S(1)}, s32[4]{0:T(128)}, u32[]{:S(2)}) copy-start(s32[4]{0:T(128)} %index_ref.1) | copy-start | bytes 52
